TPU v7x, 32 devices: a whole 2x2x4 slice. The times are simulated.
32 devices in a mesh: groups: 2 (over y), row: 4 (over x, core), col: 4 (over z).
Axes of the slice: x: 2, y: 2, z: 4, core: 2. Of those that a mesh axis runs over, the one named last changes fastest.
Arguments:
- tiles: float32 [512, 128, 128], P(('groups', 'row', 'col')), parts along dimension 0, may hold values from 0 to 9
- tile_index: int32 [512, 2], P(('groups', 'row', 'col')), parts along dimension 0, may hold values from 0 to 3, as said below
- tile_count: int32 [32], P(('groups', 'row', 'col')), parts along dimension 0, may hold values from 4 to 16, as said below
- sources: int32 [16], P('groups'), parts along dimension 0, may hold values from 0 to 2047
Outputs:
- distance: float32 [16, 2048], P('groups', ('row', 'col')), parts along dimension 0
- path_counts: float32 [16, 2048], P('groups', ('row', 'col')), parts along dimension 0
- centrality: float32 [4096], P(('groups', 'row', 'col')), parts along dimension 0
There are 2 independent parts, one for each index of `groups`. A program takes and returns all parts, laid end to end along the dimension named above; each array names one. Nothing has to cross between parts.
Inputs may be any that keep to these rules, and one draw needn't show every extreme that they name: `tile_index`: entry (r, c) of a slot has r below 4 and c below 4; the 16 slots of one device name distinct pairs. `tile_count`: one entry per device; slots of a device from its count on hold only zeros; some device has all 16 slots live.
All inputs are finite; a program needn't handle non-finite values.
Results may differ from a plain program's by a relative error of at most 0.0003.
Values sent between devices are 32-bit elements; how exact they have to be, the bound alone decides.
A program may use at most 64 MiB of HBM per device.

v0:
```python
import jax
import jax.numpy as jnp
from jax import lax
from jax.sharding import PartitionSpec as P

LEVELS = 3
BACK = 2
far_value = 1000000.0
no_edge = 2000000.0


def combined_all(value, axis, join):
    pieces = jax.tree.map(lambda part: lax.all_gather(part, axis), value)
    head = jax.tree.map(lambda part: part[0], pieces)
    tail = jax.tree.map(lambda part: part[1:], pieces)
    running, _ = lax.scan(lambda running, piece: (join(running, piece), None), head, tail)
    return running


def combine_pair(left_pair, right_pair):
    best_dist = jnp.minimum(left_pair[0], right_pair[0])
    total_count = jnp.where(left_pair[0] == best_dist, left_pair[1], 0.0) + jnp.where(
        right_pair[0] == best_dist, right_pair[1], 0.0
    )
    return (best_dist, total_count)


def pick_rows(band, tile_ids, tile_side):
    source_rows = band.shape[0]
    shaped = band.reshape(source_rows, band.shape[1] // tile_side, tile_side)
    return jnp.take(shaped, tile_ids, axis=1).transpose(1, 0, 2)


def split_blocks(values, tile_side):
    block_size = min(16, tile_side)
    blocks = tile_side // block_size
    return values.reshape(values.shape[0], values.shape[1], blocks, block_size).transpose(
        2, 0, 1, 3
    )


def weight_blocks(weights, tile_side):
    block_size = min(16, tile_side)
    blocks = tile_side // block_size
    return weights.reshape(weights.shape[0], blocks, block_size, tile_side).transpose(1, 0, 2, 3)


def relax_group(near_dist, near_count, weights):
    group, source_rows, tile_side = near_dist.shape

    def advance(carried, pieces):
        dist_part, count_part, weight_part = pieces
        reached = dist_part[:, :, :, None] + weight_part[:, None, :, :]
        best_dist = jnp.min(reached, axis=2)
        total_count = jnp.sum(
            jnp.where(reached == best_dist[:, :, None, :], count_part[:, :, :, None], 0.0), axis=2
        )
        return (combine_pair(carried, (best_dist, total_count)), None)

    initial = (
        jnp.full((group, source_rows, tile_side), far_value, jnp.float32),
        jnp.zeros((group, source_rows, tile_side), jnp.float32),
    )
    result, unused = lax.scan(
        advance,
        initial,
        (
            split_blocks(near_dist, tile_side),
            split_blocks(near_count, tile_side),
            weight_blocks(weights, tile_side),
        ),
    )
    return result


def depend_group(upper_dist, lower_dist, lower_coef, weights):
    group, source_rows, tile_side = upper_dist.shape

    def dependency_rows(pieces):
        upper_part, weight_part = pieces
        reached = upper_part[:, :, :, None] + weight_part[:, None, :, :]
        return jnp.sum(
            jnp.where(reached == lower_dist[:, :, None, :], lower_coef[:, :, None, :], 0.0), axis=3
        )

    row_parts = lax.map(
        dependency_rows, (split_blocks(upper_dist, tile_side), weight_blocks(weights, tile_side))
    )
    return row_parts.transpose(1, 2, 0, 3).reshape(group, source_rows, tile_side)


def per_device(tiles, tile_index, tile_count, sources):
    tile_side = tiles.shape[1]
    slot_total = tiles.shape[0]
    source_rows = sources.shape[0]
    row_count = lax.axis_size("row")
    col_count = lax.axis_size("col")
    my_row = lax.axis_index("row")
    my_col = lax.axis_index("col")
    own_ids = (my_row * col_count + my_col) * tile_side + jnp.arange(tile_side, dtype=jnp.int32)
    own_source = own_ids[None, :] == sources[:, None]
    band_ids = my_row * col_count * tile_side + jnp.arange(col_count * tile_side, dtype=jnp.int32)
    band_source = band_ids[None, :] == sources[:, None]
    live_count = tile_count[0]
    start_dist = jnp.where(own_source, 0.0, far_value).astype(jnp.float32)
    source_ones = jnp.where(own_source, 1.0, 0.0).astype(jnp.float32)
    band_dist = jnp.where(band_source, 0.0, far_value).astype(jnp.float32)
    band_paths = jnp.where(band_source, 1.0, 0.0).astype(jnp.float32)

    def group_parts(start, width):
        slot_ids = start + jnp.arange(width, dtype=jnp.int32)
        live = slot_ids < live_count
        weights = jnp.where((tiles > 0) & live[:, None, None], tiles, no_edge)
        return (weights, tile_index, live)

    def run_groups(process, initial):
        return process(0, slot_total, initial)

    def gather_band(dist_part, path_part):
        return (
            lax.all_gather(dist_part, "col", axis=1, tiled=True),
            lax.all_gather(path_part, "col", axis=1, tiled=True),
        )

    column_tiles = jnp.arange(row_count, dtype=jnp.int32)
    row_tiles = jnp.arange(col_count, dtype=jnp.int32)
    own_dist = start_dist
    own_paths = source_ones
    for level_no in range(LEVELS):
        if level_no > 0:
            band_dist, band_paths = gather_band(own_dist, own_paths)

        def forward_group(start, width, carried, band_dist=band_dist, band_paths=band_paths):
            weights, places, live = group_parts(start, width)
            near_dist = pick_rows(band_dist, places[:, 0], tile_side)
            near_count = pick_rows(band_paths, places[:, 0], tile_side)
            found_dist, found_count = relax_group(near_dist, near_count, weights)
            hits = (places[None, :, 1] == column_tiles[:, None]) & live[None, :]
            masked = jnp.where(hits[:, :, None, None], found_dist[None], far_value)
            best_dist = jnp.min(masked, axis=1)
            total_count = jnp.sum(
                jnp.where(
                    hits[:, :, None, None] & (found_dist[None] == best_dist[:, None]),
                    found_count[None],
                    0.0,
                ),
                axis=1,
            )
            return combine_pair(carried, (best_dist, total_count))

        initial = (
            jnp.full((row_count, source_rows, tile_side), far_value, jnp.float32),
            jnp.zeros((row_count, source_rows, tile_side), jnp.float32),
        )
        folded_dist, folded_count = run_groups(forward_group, initial)
        partial_dist = folded_dist.transpose(1, 0, 2).reshape(source_rows, row_count * tile_side)
        partial_count = folded_count.transpose(1, 0, 2).reshape(source_rows, row_count * tile_side)
        merged = combined_all((partial_dist, partial_count), "row", combine_pair)
        found_dist = lax.dynamic_slice_in_dim(merged[0], my_row * tile_side, tile_side, 1)
        found_count = lax.dynamic_slice_in_dim(merged[1], my_row * tile_side, tile_side, 1)
        own_dist = jnp.minimum(start_dist, found_dist)
        own_paths = source_ones + jnp.where(found_dist == own_dist, found_count, 0.0)
    band_dist, band_paths = gather_band(own_dist, own_paths)
    dependency = jnp.zeros((source_rows, tile_side), jnp.float32)
    for back_no in range(BACK):
        coefficient = jnp.where(
            own_paths > 0.5, (1.0 + dependency) / jnp.maximum(own_paths, 1.0), 0.0
        )
        lower_all, coef_all = (
            lax.all_gather(own_dist, "row", axis=1, tiled=True),
            lax.all_gather(coefficient, "row", axis=1, tiled=True),
        )

        def backward_group(start, width, carried, lower_all=lower_all, coef_all=coef_all):
            weights, places, live = group_parts(start, width)
            upper_dist = pick_rows(band_dist, places[:, 0], tile_side)
            lower_dist = pick_rows(lower_all, places[:, 1], tile_side)
            lower_coef = pick_rows(coef_all, places[:, 1], tile_side)
            dep_terms = depend_group(upper_dist, lower_dist, lower_coef, weights)
            hits = (places[None, :, 0] == row_tiles[:, None]) & live[None, :]
            return carried + jnp.sum(
                jnp.where(hits[:, :, None, None], dep_terms[None], 0.0), axis=1
            )

        folded = run_groups(
            backward_group, jnp.zeros((col_count, source_rows, tile_side), jnp.float32)
        )
        accumulated = folded.transpose(1, 0, 2).reshape(source_rows, col_count * tile_side)
        summed = lax.psum_scatter(accumulated, "col", scatter_dimension=1, tiled=True)
        dependency = own_paths * summed
    centrality = jnp.sum(jnp.where(own_source, 0.0, dependency), axis=0) / source_rows
    shown = jnp.where(own_dist < 0.5 * far_value, own_dist, -1.0)
    return (shown, own_paths, centrality)


def solution(mesh):
    in_specs = (
        P(("groups", "row", "col"), None, None),
        P(("groups", "row", "col"), None),
        P(("groups", "row", "col")),
        P("groups"),
    )
    out_specs = (
        P("groups", ("row", "col")),
        P("groups", ("row", "col")),
        P(("groups", "row", "col")),
    )
    return jax.shard_map(
        per_device, mesh=mesh, in_specs=in_specs, out_specs=out_specs, check_vma=False
    )
```

profile of v0, /device:TPU:0, one launch (start us, length us, event | category | flops | bytes accessed | tf_op | source)
XLA Modules:
  0.0 230.2 jit_solution(145529615375615002)
XLA Ops:
  7.2 0.8 compare_and_fusion
  8.0 0.8 slice_bitcast_fusion.6
  8.8 0.7 compare_select_fusion
  12.1 9.8 %while.100 = (s32[]{:T(128)}, f32[16,8,128]{2,1,0:T(8,128)S(1)}, f32[16,8,128]{2,1,0:T(8,128)S(1)}, f32[8,16,8,16]{3,0,2,1:T(8,128)S(1)}, f32[8,16,16,128]{3,2,1...) while((s32[]{:T(128)}, f32[16,8,128]{2,1,0:T(8,128)S(1)}, ...), condition=%wide.region_3.5_spmd.clone, body=%wide.region_0.4_spmd.clone.sunk | while | flops 1671171 | bytes 1171559 | solution.py:64
  12.7 0.6 select_reduce_fusion.20
  13.9 0.6 select_reduce_fusion.20
  15.1 0.6 select_reduce_fusion.20
  16.4 0.6 select_reduce_fusion.20
  17.6 0.6 select_reduce_fusion.20
  18.8 0.6 select_reduce_fusion.20
  20.0 0.6 select_reduce_fusion.20
  21.3 0.6 select_reduce_fusion.20
  22.3 6.2 %all_gather.44 = f32[4,8,512]{2,1,0:T(8,128)S(1)} all-gather(f32[1,8,512]{2,1,0:T(8,128)S(1)} %get-tuple-element.541), channel_id=1, replica_groups=mesh['groups'=2,'row'=4,'col'=4] {'row'}, dimensions={0}, use_global_device_ids=true | all-gather | bytes 81920 | tf_op jit(solution)/shard_map/all_gather | solution.py:13
  29.1 5.5 %all_gather.43 = f32[4,8,512]{2,1,0:T(8,128)S(1)} all-gather(f32[1,8,512]{2,1,0:T(8,128)S(1)} %get-tuple-element.542), channel_id=1, replica_groups=mesh['groups'=2,'row'=4,'col'=4] {'row'}, dimensions={0}, use_global_device_ids=true | all-gather | bytes 81920 | tf_op jit(solution)/shard_map/all_gather | solution.py:13
  34.7 0.8 slice-done
  35.5 0.6 copy-done.5
  36.3 13.6 %all_gather.45 = f32[8,512]{1,0:T(8,128)S(1)} all-gather(f32[8,128]{1,0:T(8,128)S(1)} %get-tuple-element.536), channel_id=1, replica_groups=mesh['groups'=2,'row'=4,'col'=4] {'col'}, dimensions={1}, use_global_device_ids=true | all-gather | bytes 20480 | tf_op jit(solution)/shard_map/all_gather | solution.py:121
  50.5 13.2 %all_gather.46 = f32[8,512]{1,0:T(8,128)S(1)} all-gather(f32[8,128]{1,0:T(8,128)S(1)} %get-tuple-element.535), channel_id=1, replica_groups=mesh['groups'=2,'row'=4,'col'=4] {'col'}, dimensions={1}, use_global_device_ids=true | all-gather | bytes 20480 | tf_op jit(solution)/shard_map/all_gather | solution.py:122
  64.7 9.8 %while.101 = (s32[]{:T(128)}, f32[16,8,128]{2,1,0:T(8,128)S(1)}, f32[16,8,128]{2,1,0:T(8,128)S(1)}, f32[8,16,8,16]{3,0,2,1:T(8,128)S(1)}, f32[8,16,16,128]{3,2,1...) while((s32[]{:T(128)}, f32[16,8,128]{2,1,0:T(8,128)S(1)}, ...), condition=%wide.region_11.13_spmd.clone, body=%wide.region_8.12_spmd.clone.sunk | while | flops 1671171 | bytes 1171559 | solution.py:64
  65.3 0.6 select_reduce_fusion.21
  66.5 0.6 select_reduce_fusion.21
  67.7 0.6 select_reduce_fusion.21
  68.9 0.6 select_reduce_fusion.21
  70.2 0.6 select_reduce_fusion.21
  71.4 0.6 select_reduce_fusion.21
  72.6 0.6 select_reduce_fusion.21
  74.8 5.2 %all_gather.48 = f32[4,8,512]{2,1,0:T(8,128)S(1)} all-gather(f32[1,8,512]{2,1,0:T(8,128)S(1)} %get-tuple-element.539), channel_id=1, replica_groups=mesh['groups'=2,'row'=4,'col'=4] {'row'}, dimensions={0}, use_global_device_ids=true | all-gather | bytes 81920 | tf_op jit(solution)/shard_map/all_gather | solution.py:13
  80.7 5.2 %all_gather.47 = f32[4,8,512]{2,1,0:T(8,128)S(1)} all-gather(f32[1,8,512]{2,1,0:T(8,128)S(1)} %get-tuple-element.540), channel_id=1, replica_groups=mesh['groups'=2,'row'=4,'col'=4] {'row'}, dimensions={0}, use_global_device_ids=true | all-gather | bytes 81920 | tf_op jit(solution)/shard_map/all_gather | solution.py:13
  86.0 0.8 slice-done.1
  86.9 13.2 %all_gather.49 = f32[8,512]{1,0:T(8,128)S(1)} all-gather(f32[8,128]{1,0:T(8,128)S(1)} %get-tuple-element.534), channel_id=1, replica_groups=mesh['groups'=2,'row'=4,'col'=4] {'col'}, dimensions={1}, use_global_device_ids=true | all-gather | bytes 20480 | tf_op jit(solution)/shard_map/all_gather | solution.py:121
  100.7 13.2 %all_gather.50 = f32[8,512]{1,0:T(8,128)S(1)} all-gather(f32[8,128]{1,0:T(8,128)S(1)} %get-tuple-element.533), channel_id=1, replica_groups=mesh['groups'=2,'row'=4,'col'=4] {'col'}, dimensions={1}, use_global_device_ids=true | all-gather | bytes 20480 | tf_op jit(solution)/shard_map/all_gather | solution.py:122
  114.9 9.8 %while.102 = (s32[]{:T(128)}, f32[16,8,128]{2,1,0:T(8,128)S(1)}, f32[16,8,128]{2,1,0:T(8,128)S(1)}, f32[8,16,8,16]{3,0,2,1:T(8,128)S(1)}, f32[8,16,16,128]{3,2,1...) while((s32[]{:T(128)}, f32[16,8,128]{2,1,0:T(8,128)S(1)}, ...), condition=%wide.region_19.21_spmd.clone, body=%wide.region_16.20_spmd.clone.sunk | while | flops 1671171 | bytes 1171559 | solution.py:64
  122.8 0.6 select_reduce_fusion.22
  125.0 5.2 %all_gather.52 = f32[4,8,512]{2,1,0:T(8,128)S(1)} all-gather(f32[1,8,512]{2,1,0:T(8,128)S(1)} %get-tuple-element.537), channel_id=1, replica_groups=mesh['groups'=2,'row'=4,'col'=4] {'row'}, dimensions={0}, use_global_device_ids=true | all-gather | bytes 81920 | tf_op jit(solution)/shard_map/all_gather | solution.py:13
  130.9 5.2 %all_gather.51 = f32[4,8,512]{2,1,0:T(8,128)S(1)} all-gather(f32[1,8,512]{2,1,0:T(8,128)S(1)} %get-tuple-element.538), channel_id=1, replica_groups=mesh['groups'=2,'row'=4,'col'=4] {'row'}, dimensions={0}, use_global_device_ids=true | all-gather | bytes 81920 | tf_op jit(solution)/shard_map/all_gather | solution.py:13
  136.1 0.8 slice-done.2
  137.1 13.2 %all_gather.53 = f32[8,512]{1,0:T(8,128)S(1)} all-gather(f32[8,128]{1,0:T(8,128)S(1)} %get-tuple-element.522), channel_id=1, replica_groups=mesh['groups'=2,'row'=4,'col'=4] {'col'}, dimensions={1}, use_global_device_ids=true | all-gather | bytes 20480 | tf_op jit(solution)/shard_map/all_gather | solution.py:121
  150.3 5.2 %all_gather.54 = f32[8,512]{1,0:T(8,128)S(1)} all-gather(f32[8,128]{1,0:T(8,128)S(1)} %get-tuple-element.522), channel_id=1, replica_groups=mesh['groups'=2,'row'=4,'col'=4] {'row'}, dimensions={1}, use_global_device_ids=true | all-gather | bytes 20480 | tf_op jit(solution)/shard_map/all_gather | solution.py:170
  156.1 5.2 %all_gather.55 = f32[8,512]{1,0:T(8,128)S(1)} all-gather(f32[8,128]{1,0:T(8,128)S(1)} %get-tuple-element.520), channel_id=1, replica_groups=mesh['groups'=2,'row'=4,'col'=4] {'row'}, dimensions={1}, use_global_device_ids=true | all-gather | bytes 20480 | tf_op jit(solution)/shard_map/all_gather | solution.py:171
  162.9 6.1 %while.98 = (s32[]{:T(128)}, f32[8,16,8,16]{3,2,1,0:T(8,128)S(1)}, f32[8,16,8,16]{3,2,1,0:T(8,128)S(1)}, f32[8,16,16,128]{3,2,1,0:T(8,128)S(1)}, f32[16,8,128]{2...) while((s32[]{:T(128)}, f32[8,16,8,16]{3,2,1,0:T(8,128)S(1)}, f32[8,16,8,16]{3,2,1,0:T(8,128)S(1)}, ...), condition=%wide.region_26.28_spmd, body=%wide.region_24.27_spmd.sunk | while | flops 1046530 | bytes 688217 | solution.py:86
  162.9 0.7 select_reduce_fusion.18
  163.7 0.7 select_reduce_fusion.18
  164.5 0.7 select_reduce_fusion.18
  165.2 0.7 select_reduce_fusion.18
  166.0 0.7 select_reduce_fusion.18
  166.7 0.7 select_reduce_fusion.18
  167.5 0.7 select_reduce_fusion.18
  168.3 0.7 select_reduce_fusion.18
  169.5 0.7 select_reduce_fusion.6
  170.3 20.4 %reduce-scatter.3.cloned.1.call-done = f32[8,128]{1,0:T(8,128)} async-done(((f32[8,512]{1,0:T(8,128)}), f32[8,128]{1,0:T(8,128)}) %reduce-scatter.3.cloned.1.call-update) | async-done | bytes 4112 | tf_op jit(solution)/shard_map/reduce_scatter | solution.py:189
  190.7 0.7 divide_select_fusion
  191.3 5.2 %all_gather.56 = f32[8,512]{1,0:T(8,128)S(1)} all-gather(f32[8,128]{1,0:T(8,128)S(1)} %divide_select_fusion), channel_id=1, replica_groups=mesh['groups'=2,'row'=4,'col'=4] {'row'}, dimensions={1}, use_global_device_ids=true | all-gather | bytes 20480 | tf_op jit(solution)/shard_map/all_gather | solution.py:171
  197.2 6.1 %while.99 = (s32[]{:T(128)}, f32[8,16,8,16]{3,2,1,0:T(8,128)S(1)}, f32[8,16,8,16]{3,2,1,0:T(8,128)S(1)}, f32[8,16,16,128]{3,2,1,0:T(8,128)S(1)}, f32[16,8,128]{2...) while((s32[]{:T(128)}, f32[8,16,8,16]{3,2,1,0:T(8,128)S(1)}, f32[8,16,8,16]{3,2,1,0:T(8,128)S(1)}, ...), condition=%wide.region_31.33_spmd, body=%wide.region_29.32_spmd.sunk | while | flops 1046530 | bytes 688217 | solution.py:86
  197.3 0.7 select_reduce_fusion.19
  198.1 0.7 select_reduce_fusion.19
  198.8 0.7 select_reduce_fusion.19
  199.6 0.7 select_reduce_fusion.19
  200.4 0.7 select_reduce_fusion.19
  201.1 0.7 select_reduce_fusion.19
  201.9 0.7 select_reduce_fusion.19
  202.6 0.7 select_reduce_fusion.19
  203.9 0.7 select_reduce_fusion.5
  205.2 16.9 %reduce-scatter.5.cloned.1.call-done = f32[8,128]{1,0:T(8,128)} async-done(((f32[8,512]{1,0:T(8,128)}), f32[8,128]{1,0:T(8,128)}) %reduce-scatter.5.cloned.1.call-update) | async-done | bytes 4112 | tf_op jit(solution)/shard_map/reduce_scatter | solution.py:189
  222.1 0.8 fusion.12
  (248 shorter events, 32.3 us)
Async XLA Ops:
  7.2 4.7 %copy-start = (f32[16,128,128]{2,1,0:T(8,128)S(1)}, f32[16,128,128]{2,1,0:T(8,128)}, u32[]{:S(2)}) copy-start(f32[16,128,128]{2,1,0:T(8,128)} %param.22) | copy-start | bytes 3145732
  7.2 183.5 %reduce-scatter.3.cloned.1.call-start = ((), (), s32[]{:S(2)}) async-start(), calls=%async_computation.2 | async-start | bytes 20480 | tf_op jit(solution)/shard_map/reduce_scatter | solution.py:189
  28.5 0.6 copy-start.1
  34.6 0.8 slice-start
  35.5 0.7 copy-start.5
  80.1 0.6 copy-start.2
  85.9 0.8 slice-start.1
  130.3 0.6 copy-start.3
  136.1 0.8 slice-start.2
  137.1 85.0 %copy-start.4 = (f32[8,128]{1,0:T(8,128)}, f32[8,128]{1,0:T(8,128)S(1)}, u32[]{:S(2)}) copy-start(f32[8,128]{1,0:T(8,128)S(1)} %get-tuple-element.521) | copy-start | bytes 12292
  170.3 51.9 %reduce-scatter.5.cloned.1.call-start = ((), (), s32[]{:S(2)}) async-start(), calls=%async_computation.3 | async-start | bytes 20480 | tf_op jit(solution)/shard_map/reduce_scatter | solution.py:189
Sparse Core Ops, SparseCore 0:
  170.4 20.2 reduce-scatter.2
  204.7 17.3 reduce-scatter.4
where the time goes:
time: 231 us; the launch traced here: 230 us
  blocking collectives  115 us (50%)
  other arithmetic  43.7 us (19%)
  waiting for transfers between devices  37.3 us (16%)
  local copies, waits for them, and re-layouts  17.2 us (7%)
  between operations  15.2 us (7%)
    all_gather x3, blocking collectives, gather_band(): lax.all_gather(dist_part, 'col', axis=1, tiled=True)  40 us
    reduce_scatter x2, waiting for transfers between devices, per_device(): lax.psum_scatter(accumulated, 'col', scatter_dimension=1, tiled=True)  37.3 us
    all_gather x6, blocking collectives, combined_all(): pieces = jax.tree.map(lambda part: lax.all_gather(part, axis), value)  32.6 us
    all_gather x2, blocking collectives, gather_band(): lax.all_gather(path_part, 'col', axis=1, tiled=True)  26.4 us
    reduce_sum x24, other arithmetic, advance(): jnp.sum(jnp.where(reached == best_dist[:, :, None, :], count_part[:, :, :...  14.9 us
    reduce_sum x16, other arithmetic, dependency_rows(): jnp.sum(jnp.where(reached == lower_dist[:, :, None, :], lower_coef[:, :,...  10.9 us
    all_gather x2, blocking collectives, per_device(): lax.all_gather(coefficient, 'row', axis=1, tiled=True)  10.4 us
    reduce_min x24, other arithmetic, advance(): best_dist = jnp.min(reached, axis=2)  9.06 us
  transfers between devices with their start and end apart: 2, of which 2 were waited for; matrix products, arithmetic and copies ran while one was open for 0% of the time, Pallas kernels for 0%

commit v1 on v0

--- a/solution.py
+++ b/solution.py
@@ -1,3 +1,4 @@
+import functools
 import jax
 import jax.numpy as jnp
 from jax import lax
@@ -7,6 +8,14 @@
 BACK = 2
 far_value = 1000000.0
 no_edge = 2000000.0
+
+
+def try_all_the_outputs(frame_in, mesh_name, row_dim):
+    piece_out = jnp.concatenate(lax.all_gather(frame_in, axis_name=mesh_name), axis=row_dim)
+    return piece_out
+
+
+choose_the_heaps = functools.partial(try_all_the_outputs, mesh_name="col", row_dim=1)
 
 
 def combined_all(value, axis, join):
@@ -117,10 +126,7 @@
         return process(0, slot_total, initial)
 
     def gather_band(dist_part, path_part):
-        return (
-            lax.all_gather(dist_part, "col", axis=1, tiled=True),
-            lax.all_gather(path_part, "col", axis=1, tiled=True),
-        )
+        return (lax.all_gather(dist_part, "col", axis=1, tiled=True), choose_the_heaps(path_part))
 
     column_tiles = jnp.arange(row_count, dtype=jnp.int32)
     row_tiles = jnp.arange(col_count, dtype=jnp.int32)

time: 231 us -> 231 us (level)
  no operation moved by 1% of the time
where the time goes in v1:
time: 231 us; the launch traced here: 230 us
  blocking collectives  115 us (50%)
  other arithmetic  43.7 us (19%)
  waiting for transfers between devices  37.3 us (16%)
  local copies, waits for them, and re-layouts  17.2 us (7%)
  between operations  15.2 us (7%)
    all_gather x3, blocking collectives, gather_band(): lax.all_gather(dist_part, 'col', axis=1, tiled=True)  40 us
    reduce_scatter x2, waiting for transfers between devices, per_device(): lax.psum_scatter(accumulated, 'col', scatter_dimension=1, tiled=True)  37.3 us
    all_gather x6, blocking collectives, combined_all(): pieces = jax.tree.map(lambda part: lax.all_gather(part, axis), value)  32.6 us
    all_gather x2, blocking collectives, try_all_the_outputs(): lax.all_gather(frame_in, axis_name=mesh_name)  26.4 us
    reduce_sum x24, other arithmetic, advance(): jnp.sum(jnp.where(reached == best_dist[:, :, None, :], count_part[:, :, :...  14.9 us
    reduce_sum x16, other arithmetic, dependency_rows(): jnp.sum(jnp.where(reached == lower_dist[:, :, None, :], lower_coef[:, :,...  10.9 us
    all_gather x2, blocking collectives, per_device(): lax.all_gather(coefficient, 'row', axis=1, tiled=True)  10.4 us
    reduce_min x24, other arithmetic, advance(): best_dist = jnp.min(reached, axis=2)  9.06 us
  transfers between devices with their start and end apart: 2, of which 2 were waited for; matrix products, arithmetic and copies ran while one was open for 0% of the time, Pallas kernels for 0%

profile of v1, /device:TPU:0, one launch (start us, length us, event | category | flops | bytes accessed | tf_op | source)
XLA Modules:
  0.0 230.2 jit_solution(4931143357158498832)
XLA Ops:
  7.2 0.8 compare_and_fusion
  8.0 0.8 slice_bitcast_fusion.6
  8.8 0.7 compare_select_fusion
  12.1 9.8 %while.100 = (s32[]{:T(128)}, f32[16,8,128]{2,1,0:T(8,128)S(1)}, f32[16,8,128]{2,1,0:T(8,128)S(1)}, f32[8,16,8,16]{3,0,2,1:T(8,128)S(1)}, f32[8,16,16,128]{3,2,1...) while((s32[]{:T(128)}, f32[16,8,128]{2,1,0:T(8,128)S(1)}, ...), condition=%wide.region_3.5_spmd.clone, body=%wide.region_0.4_spmd.clone.sunk | while | flops 1671171 | bytes 1171559 | solution.py:73
  12.7 0.6 select_reduce_fusion.20
  13.9 0.6 select_reduce_fusion.20
  15.1 0.6 select_reduce_fusion.20
  16.4 0.6 select_reduce_fusion.20
  17.6 0.6 select_reduce_fusion.20
  18.8 0.6 select_reduce_fusion.20
  20.0 0.6 select_reduce_fusion.20
  21.3 0.6 select_reduce_fusion.20
  22.3 6.2 %all_gather.50 = f32[4,8,512]{2,1,0:T(8,128)S(1)} all-gather(f32[1,8,512]{2,1,0:T(8,128)S(1)} %get-tuple-element.541), channel_id=1, replica_groups=mesh['groups'=2,'row'=4,'col'=4] {'row'}, dimensions={0}, use_global_device_ids=true | all-gather | bytes 81920 | tf_op jit(solution)/shard_map/all_gather | solution.py:22
  29.1 5.5 %all_gather.49 = f32[4,8,512]{2,1,0:T(8,128)S(1)} all-gather(f32[1,8,512]{2,1,0:T(8,128)S(1)} %get-tuple-element.542), channel_id=1, replica_groups=mesh['groups'=2,'row'=4,'col'=4] {'row'}, dimensions={0}, use_global_device_ids=true | all-gather | bytes 81920 | tf_op jit(solution)/shard_map/all_gather | solution.py:22
  34.7 0.8 slice-done
  35.5 0.6 copy-done.5
  36.3 13.6 %all_gather.51 = f32[8,512]{1,0:T(8,128)S(1)} all-gather(f32[8,128]{1,0:T(8,128)S(1)} %get-tuple-element.536), channel_id=1, replica_groups=mesh['groups'=2,'row'=4,'col'=4] {'col'}, dimensions={1}, use_global_device_ids=true | all-gather | bytes 20480 | tf_op jit(solution)/shard_map/all_gather | solution.py:129
  50.5 13.2 %all-gather = f32[32,128]{1,0:T(8,128)S(1)} all-gather(f32[8,128]{1,0:T(8,128)S(1)} %get-tuple-element.535), channel_id=2, replica_groups=mesh['groups'=2,'row'=4,'col'=4] {'col'}, dimensions={0}, use_global_device_ids=true | all-gather | bytes 20480 | tf_op jit(solution)/shard_map/all_gather | solution.py:14
  64.7 9.8 %while.101 = (s32[]{:T(128)}, f32[16,8,128]{2,1,0:T(8,128)S(1)}, f32[16,8,128]{2,1,0:T(8,128)S(1)}, f32[8,16,8,16]{3,0,2,1:T(8,128)S(1)}, f32[8,16,16,128]{3,2,1...) while((s32[]{:T(128)}, f32[16,8,128]{2,1,0:T(8,128)S(1)}, ...), condition=%wide.region_11.13_spmd.clone, body=%wide.region_8.12_spmd.clone.sunk | while | flops 1671171 | bytes 1171559 | solution.py:73
  65.3 0.6 select_reduce_fusion.21
  66.5 0.6 select_reduce_fusion.21
  67.7 0.6 select_reduce_fusion.21
  68.9 0.6 select_reduce_fusion.21
  70.2 0.6 select_reduce_fusion.21
  71.4 0.6 select_reduce_fusion.21
  72.6 0.6 select_reduce_fusion.21
  74.8 5.2 %all_gather.55 = f32[4,8,512]{2,1,0:T(8,128)S(1)} all-gather(f32[1,8,512]{2,1,0:T(8,128)S(1)} %get-tuple-element.539), channel_id=1, replica_groups=mesh['groups'=2,'row'=4,'col'=4] {'row'}, dimensions={0}, use_global_device_ids=true | all-gather | bytes 81920 | tf_op jit(solution)/shard_map/all_gather | solution.py:22
  80.7 5.2 %all_gather.54 = f32[4,8,512]{2,1,0:T(8,128)S(1)} all-gather(f32[1,8,512]{2,1,0:T(8,128)S(1)} %get-tuple-element.540), channel_id=1, replica_groups=mesh['groups'=2,'row'=4,'col'=4] {'row'}, dimensions={0}, use_global_device_ids=true | all-gather | bytes 81920 | tf_op jit(solution)/shard_map/all_gather | solution.py:22
  86.0 0.8 slice-done.1
  86.9 13.2 %all_gather.56 = f32[8,512]{1,0:T(8,128)S(1)} all-gather(f32[8,128]{1,0:T(8,128)S(1)} %get-tuple-element.534), channel_id=1, replica_groups=mesh['groups'=2,'row'=4,'col'=4] {'col'}, dimensions={1}, use_global_device_ids=true | all-gather | bytes 20480 | tf_op jit(solution)/shard_map/all_gather | solution.py:129
  100.7 13.2 %all-gather.1 = f32[32,128]{1,0:T(8,128)S(1)} all-gather(f32[8,128]{1,0:T(8,128)S(1)} %get-tuple-element.533), channel_id=3, replica_groups=mesh['groups'=2,'row'=4,'col'=4] {'col'}, dimensions={0}, use_global_device_ids=true | all-gather | bytes 20480 | tf_op jit(solution)/shard_map/all_gather | solution.py:14
  114.9 9.8 %while.102 = (s32[]{:T(128)}, f32[16,8,128]{2,1,0:T(8,128)S(1)}, f32[16,8,128]{2,1,0:T(8,128)S(1)}, f32[8,16,8,16]{3,0,2,1:T(8,128)S(1)}, f32[8,16,16,128]{3,2,1...) while((s32[]{:T(128)}, f32[16,8,128]{2,1,0:T(8,128)S(1)}, ...), condition=%wide.region_19.21_spmd.clone, body=%wide.region_16.20_spmd.clone.sunk | while | flops 1671171 | bytes 1171559 | solution.py:73
  122.8 0.6 select_reduce_fusion.22
  125.0 5.2 %all_gather.60 = f32[4,8,512]{2,1,0:T(8,128)S(1)} all-gather(f32[1,8,512]{2,1,0:T(8,128)S(1)} %get-tuple-element.537), channel_id=1, replica_groups=mesh['groups'=2,'row'=4,'col'=4] {'row'}, dimensions={0}, use_global_device_ids=true | all-gather | bytes 81920 | tf_op jit(solution)/shard_map/all_gather | solution.py:22
  130.9 5.2 %all_gather.59 = f32[4,8,512]{2,1,0:T(8,128)S(1)} all-gather(f32[1,8,512]{2,1,0:T(8,128)S(1)} %get-tuple-element.538), channel_id=1, replica_groups=mesh['groups'=2,'row'=4,'col'=4] {'row'}, dimensions={0}, use_global_device_ids=true | all-gather | bytes 81920 | tf_op jit(solution)/shard_map/all_gather | solution.py:22
  136.1 0.8 slice-done.2
  137.1 13.2 %all_gather.61 = f32[8,512]{1,0:T(8,128)S(1)} all-gather(f32[8,128]{1,0:T(8,128)S(1)} %get-tuple-element.522), channel_id=1, replica_groups=mesh['groups'=2,'row'=4,'col'=4] {'col'}, dimensions={1}, use_global_device_ids=true | all-gather | bytes 20480 | tf_op jit(solution)/shard_map/all_gather | solution.py:129
  150.3 5.2 %all_gather.62 = f32[8,512]{1,0:T(8,128)S(1)} all-gather(f32[8,128]{1,0:T(8,128)S(1)} %get-tuple-element.522), channel_id=1, replica_groups=mesh['groups'=2,'row'=4,'col'=4] {'row'}, dimensions={1}, use_global_device_ids=true | all-gather | bytes 20480 | tf_op jit(solution)/shard_map/all_gather | solution.py:176
  156.1 5.2 %all_gather.63 = f32[8,512]{1,0:T(8,128)S(1)} all-gather(f32[8,128]{1,0:T(8,128)S(1)} %get-tuple-element.520), channel_id=1, replica_groups=mesh['groups'=2,'row'=4,'col'=4] {'row'}, dimensions={1}, use_global_device_ids=true | all-gather | bytes 20480 | tf_op jit(solution)/shard_map/all_gather | solution.py:177
  162.9 6.1 %while.98 = (s32[]{:T(128)}, f32[8,16,8,16]{3,2,1,0:T(8,128)S(1)}, f32[8,16,8,16]{3,2,1,0:T(8,128)S(1)}, f32[8,16,16,128]{3,2,1,0:T(8,128)S(1)}, f32[16,8,128]{2...) while((s32[]{:T(128)}, f32[8,16,8,16]{3,2,1,0:T(8,128)S(1)}, f32[8,16,8,16]{3,2,1,0:T(8,128)S(1)}, ...), condition=%wide.region_26.28_spmd, body=%wide.region_24.27_spmd.sunk | while | flops 1046530 | bytes 688217 | solution.py:95
  162.9 0.7 select_reduce_fusion.18
  163.7 0.7 select_reduce_fusion.18
  164.5 0.7 select_reduce_fusion.18
  165.2 0.7 select_reduce_fusion.18
  166.0 0.7 select_reduce_fusion.18
  166.7 0.7 select_reduce_fusion.18
  167.5 0.7 select_reduce_fusion.18
  168.3 0.7 select_reduce_fusion.18
  169.5 0.7 select_reduce_fusion.6
  170.3 20.4 %reduce-scatter.3.cloned.1.call-done = f32[8,128]{1,0:T(8,128)} async-done(((f32[8,512]{1,0:T(8,128)}), f32[8,128]{1,0:T(8,128)}) %reduce-scatter.3.cloned.1.call-update) | async-done | bytes 4112 | tf_op jit(solution)/shard_map/reduce_scatter | solution.py:195
  190.7 0.7 divide_select_fusion
  191.3 5.2 %all_gather.64 = f32[8,512]{1,0:T(8,128)S(1)} all-gather(f32[8,128]{1,0:T(8,128)S(1)} %divide_select_fusion), channel_id=1, replica_groups=mesh['groups'=2,'row'=4,'col'=4] {'row'}, dimensions={1}, use_global_device_ids=true | all-gather | bytes 20480 | tf_op jit(solution)/shard_map/all_gather | solution.py:177
  197.2 6.1 %while.99 = (s32[]{:T(128)}, f32[8,16,8,16]{3,2,1,0:T(8,128)S(1)}, f32[8,16,8,16]{3,2,1,0:T(8,128)S(1)}, f32[8,16,16,128]{3,2,1,0:T(8,128)S(1)}, f32[16,8,128]{2...) while((s32[]{:T(128)}, f32[8,16,8,16]{3,2,1,0:T(8,128)S(1)}, f32[8,16,8,16]{3,2,1,0:T(8,128)S(1)}, ...), condition=%wide.region_31.33_spmd, body=%wide.region_29.32_spmd.sunk | while | flops 1046530 | bytes 688217 | solution.py:95
  197.3 0.7 select_reduce_fusion.19
  198.1 0.7 select_reduce_fusion.19
  198.8 0.7 select_reduce_fusion.19
  199.6 0.7 select_reduce_fusion.19
  200.4 0.7 select_reduce_fusion.19
  201.1 0.7 select_reduce_fusion.19
  201.9 0.7 select_reduce_fusion.19
  202.6 0.7 select_reduce_fusion.19
  203.9 0.7 select_reduce_fusion.5
  205.2 16.9 %reduce-scatter.5.cloned.1.call-done = f32[8,128]{1,0:T(8,128)} async-done(((f32[8,512]{1,0:T(8,128)}), f32[8,128]{1,0:T(8,128)}) %reduce-scatter.5.cloned.1.call-update) | async-done | bytes 4112 | tf_op jit(solution)/shard_map/reduce_scatter | solution.py:195
  222.1 0.8 fusion.12
  (248 shorter events, 32.3 us)
Async XLA Ops:
  7.2 4.7 %copy-start = (f32[16,128,128]{2,1,0:T(8,128)S(1)}, f32[16,128,128]{2,1,0:T(8,128)}, u32[]{:S(2)}) copy-start(f32[16,128,128]{2,1,0:T(8,128)} %param.22) | copy-start | bytes 3145732
  7.2 183.5 %reduce-scatter.3.cloned.1.call-start = ((), (), s32[]{:S(2)}) async-start(), calls=%async_computation.2 | async-start | bytes 20480 | tf_op jit(solution)/shard_map/reduce_scatter | solution.py:195
  28.5 0.6 copy-start.1
  34.6 0.8 slice-start
  35.5 0.7 copy-start.5
  80.1 0.6 copy-start.2
  85.9 0.8 slice-start.1
  130.3 0.6 copy-start.3
  136.1 0.8 slice-start.2
  137.1 85.0 %copy-start.4 = (f32[8,128]{1,0:T(8,128)}, f32[8,128]{1,0:T(8,128)S(1)}, u32[]{:S(2)}) copy-start(f32[8,128]{1,0:T(8,128)S(1)} %get-tuple-element.521) | copy-start | bytes 12292
  170.3 51.9 %reduce-scatter.5.cloned.1.call-start = ((), (), s32[]{:S(2)}) async-start(), calls=%async_computation.3 | async-start | bytes 20480 | tf_op jit(solution)/shard_map/reduce_scatter | solution.py:195
Sparse Core Ops, SparseCore 0:
  170.4 20.2 reduce-scatter.2
  204.7 17.3 reduce-scatter.4
